TPU v7x, 128 devices: a whole 4x4x4 slice. The times are simulated.
128 devices in a mesh: grp: 2 (over z_lo), row: 64 (over z_hi, x, y, core).
Axes of the slice: x: 4, y: 4, z: 4 (z_hi: 2, z_lo: 2; z = z_hi * 2 + z_lo), core: 2. Of those that a mesh axis runs over, the one named last changes fastest.
Arguments:
- inputs: bfloat16 [16384, 512], P('row'), may hold values from -6 to 6
- labels: int32 [16384], P('row'), may hold values from 0 to 999
- frequencies: float32 [512, 3072], P(None, 'grp'), may hold values from -0.25 to 0.25
- phases: float32 [3072], P('grp'), may hold values from 0 to 6.2832
- weights: float32 [3072, 1000], P('grp'), may hold values from -6 to 6
Outputs:
- new_weights: float32 [3072, 1000], P('grp')
- new_residual: float32 [16384, 1000], P('row')
All inputs are finite; a program needn't handle non-finite values.
Results may differ from a plain program's by a relative error of at most 0.011.
Values sent between devices are 32-bit elements; how exact they have to be, the bound alone decides.
A program may use at most 192 MiB of HBM per device.

v0:
```python
import jax
import jax.numpy as jnp
from jax import lax
from jax.sharding import PartitionSpec as P

RIDGE = 1.0
DAMP = 0.5


def from_everyone(value, axis):
    copies = jnp.broadcast_to(value, (lax.axis_size(axis), *value.shape))
    return lax.all_to_all(copies, axis, split_axis=0, concat_axis=0, tiled=True)


def over_copies(value, axis):
    everything = from_everyone(value, axis)
    return jnp.sum(everything, axis=0)


def body(inputs, labels, frequencies, phases, weights):
    groups = lax.axis_size("grp")
    width = frequencies.shape[1]
    classes = weights.shape[1]
    scale = (2.0 / (groups * width)) ** 0.5
    arg = (
        jnp.dot(inputs.astype(jnp.float32), frequencies, precision=lax.Precision.HIGHEST)
        + phases[None, :]
    )
    phi = (scale * jnp.cos(arg)).astype(jnp.bfloat16)
    onehot = (labels[:, None] == lax.broadcasted_iota(jnp.int32, (1, classes), 1)).astype(
        jnp.float32
    )
    own = jnp.dot(phi, weights.astype(jnp.bfloat16), preferred_element_type=jnp.float32)
    prediction = over_copies(own, "grp")
    residual = onehot - prediction
    res_low = residual.astype(jnp.bfloat16)
    contract = (((0,), (0,)), ((), ()))
    gram_part = lax.dot_general(phi, phi, contract, preferred_element_type=jnp.float32)
    rhs_part = lax.dot_general(phi, res_low, contract, preferred_element_type=jnp.float32)
    gram, rhs = lax.psum((gram_part, rhs_part), "row")
    rhs = rhs - RIDGE * weights
    system = gram + RIDGE * jnp.eye(width, dtype=jnp.float32)
    factor = jnp.linalg.cholesky(system)
    solution = jax.scipy.linalg.cho_solve((factor, True), rhs)
    step = DAMP * solution
    new_weights = weights + step
    delta = jnp.dot(phi, step.astype(jnp.bfloat16), preferred_element_type=jnp.float32)
    change = over_copies(delta, "grp")
    return (new_weights, residual - change)


def solution(mesh):
    return jax.shard_map(
        body,
        mesh=mesh,
        in_specs=(P("row", None), P("row"), P(None, "grp"), P("grp"), P("grp", None)),
        out_specs=(P("grp", None), P("row", None)),
        check_vma=False,
    )
```

profile of v0, /device:TPU:31, one launch (start us, length us, event | category | flops | bytes accessed | tf_op | source)
XLA Modules:
  0.0 1430.1 jit_solution(2318205319016562998)
XLA Ops:
  9.1 8.7 fusion.7
  33.8 19.1 %all-to-all-done = f32[2,256,1000]{1,2,0:T(8,128)} async-done(((f32[2,256,1000]{1,2,0:T(8,128)}), f32[2,256,1000]{1,2,0:T(8,128)}, u32[]{:S(2)}, u32[]{:S(2)}) %all-to-all-start) | async-done | bytes 2048032 | tf_op jit(solution)/shard_map/all_to_all | solution.py:12
  58.4 687.0 %all-reduce.4.cloned.1.call-done = (f32[1536,1000]{0,1:T(8,128)}, f32[1536,1536]{0,1:T(8,128)}) async-done(((f32[1536,1000]{0,1:T(8,128)}, f32[1536,1536]{0,1:T(8,128)}), (f32[1536,1000]{0,1:T(8,128)}, f32[1536,1536]{0,1:T(8,128)})) %all-reduce.4.cloned.1.call-update) | async-done | bytes 15581200 | tf_op jit(solution)/shard_map/psum | solution.py:40
  753.7 9.9 copy.12
  763.6 12.6 fusion
  777.0 11.7 cholesky.341
  802.1 9.8 custom-call.98
  816.6 12.1 cholesky.362
  829.3 9.8 custom-call.99
  843.5 11.7 cholesky.385
  856.6 10.0 custom-call.100
  871.3 11.7 cholesky.715
  884.4 9.8 custom-call.101
  899.6 11.7 cholesky.734
  912.7 9.8 custom-call.102
  927.7 12.1 cholesky.754
  941.1 9.8 custom-call.103
  956.0 11.7 cholesky.774
  969.0 9.8 custom-call.104
  984.0 11.7 cholesky.794
  997.0 9.8 custom-call.105
  1011.5 11.9 cholesky.814
  1024.7 9.8 custom-call.106
  1038.8 11.7 cholesky.834
  1051.8 10.3 custom-call.107
  1065.9 11.7 cholesky.854
  1079.0 9.8 custom-call.108
  1091.9 11.9 cholesky.872
  1121.7 43.1 %while.1 = (s32[]{:T(128)}, f32[1536,1536]{1,0:T(8,128)}, s32[12,2]{0,1:T(2,128)S(1)}, f32[12,128,128]{2,1,0:T(8,128)}, s32[]{:T(128)}) while((s32[]{:T(128)}, f32[1536,1536]{1,0:T(8,128)}, s32[12,2]{0,1:T(2,128)S(1)}, f32[12,128,128]{2,1,0:T(8,128)}, s32[]{:T(128)}) %tuple.110), condition=%wide.while_cond, body=%wide.while_body.sunk | while | flops 2 | bytes 132205 | solution.py:44
  1164.8 118.7 %custom-call.109 = f32[12,128,128]{1,2,0:T(8,128)S(1)} custom-call(f32[12,128,128]{2,1,0:T(8,128)} %get-tuple-element.9), custom_call_target="InvertDiagBlocksLowerTriangular" | custom-call | tf_op jit(solution)/shard_map/jit(_cho_solve)/triangular_solve | solution.py:44
  1393.5 8.7 multiply_add_fusion
  1402.2 15.1 %all-to-all-done.1 = f32[2,256,1000]{1,2,0:T(8,128)} async-done(((f32[2,256,1000]{1,2,0:T(8,128)}), f32[2,256,1000]{1,2,0:T(8,128)}, u32[]{:S(2)}, u32[]{:S(2)}) %all-to-all-start.1) | async-done | bytes 2048032 | tf_op jit(solution)/shard_map/all_to_all | solution.py:12
  (253 shorter events, 277.1 us)
Async XLA Ops:
  7.2 1.9 copy-start
  17.7 0.9 copy-start.3
  22.4 6.3 copy-start.4
  23.8 29.0 %all-to-all-start = ((f32[2,256,1000]{1,2,0:T(8,128)}), f32[2,256,1000]{1,2,0:T(8,128)}, u32[]{:S(2)}, u32[]{:S(2)}) async-start(f32[2,256,1000]{1,2,0:T(8,128)} %broadcast_in_dim.10), calls=%async_computation | async-start | bytes 4096000 | tf_op jit(solution)/shard_map/all_to_all | solution.py:12
  28.6 26.1 %copy-start.14 = (s32[256]{0:T(256)S(1)}, s32[256]{0:T(256)}, u32[]{:S(2)}) copy-start(s32[256]{0:T(256)} %param.6) | copy-start | bytes 3076
  28.6 716.7 %all-reduce.4.cloned.1.call-start = ((), (), s32[]{:S(2)}) async-start(), calls=%async_computation.2 | async-start | bytes 31162368 | tf_op jit(solution)/shard_map/psum | solution.py:40
  54.7 3.6 copy-start.6
  1283.5 55.2 %copy-start.8 = (f32[12,128,128]{1,2,0:T(8,128)}, f32[12,128,128]{1,2,0:T(8,128)S(1)}, u32[]{:S(2)}) copy-start(f32[12,128,128]{1,2,0:T(8,128)S(1)} %custom-call.109) | copy-start | bytes 2359300
  1283.5 6.1 copy-start.2
  1288.6 8.0 slice-start
  1291.9 4.8 slice-start.1
  1296.6 9.8 copy-start.10
  1300.2 1.5 copy-start.7
  1339.7 5.1 copy-start.9
  1348.7 3.8 copy-start.13
  1352.5 4.0 copy-start.12
  1359.9 1.5 copy-start.11
  1384.6 2.7 copy-start.5
  1388.7 28.7 %all-to-all-start.1 = ((f32[2,256,1000]{1,2,0:T(8,128)}), f32[2,256,1000]{1,2,0:T(8,128)}, u32[]{:S(2)}, u32[]{:S(2)}) async-start(f32[2,256,1000]{1,2,0:T(8,128)} %broadcast_in_dim.11), calls=%async_computation.1 | async-start | bytes 4096000 | tf_op jit(solution)/shard_map/all_to_all | solution.py:12
  1393.5 29.3 %copy-start.1 = (f32[512,1536]{1,0:T(8,128)S(1)}, f32[512,1536]{1,0:T(8,128)}, u32[]{:S(2)}) copy-start(f32[512,1536]{1,0:T(8,128)} %param.7) | copy-start | bytes 9437188
Sparse Core Ops, SparseCore 0:
  58.5 686.8 all-reduce.3
where the time goes:
time: 1440 us; the launch traced here: 1430 us
  waiting for transfers between devices  721 us (50%)
  other arithmetic  437 us (30%)
  matrix products  169 us (12%)
  local copies, waits for them, and re-layouts  70.1 us (5%)
  between operations  23.2 us (2%)
    psum x1, waiting for transfers between devices, body(): gram, rhs = lax.psum((gram_part, rhs_part), 'row')  687 us
    another operation x46, other arithmetic, body(): factor = jnp.linalg.cholesky(system)  265 us
    another operation x3, other arithmetic, body(): solution = jax.scipy.linalg.cho_solve((factor, True), rhs)  127 us
    another operation x46, matrix products, body(): solution = jax.scipy.linalg.cho_solve((factor, True), rhs)  96 us
    another operation x22, matrix products, body(): factor = jnp.linalg.cholesky(system)  50.5 us
    another operation x36, local copies, waits for them, and re-layouts  43 us
    all_to_all x2, waiting for transfers between devices, from_everyone(): return lax.all_to_all(copies, axis, split_axis=0, concat_axis=0, tiled=True)  34.2 us
  transfers between devices with their start and end apart: 3, of which 3 were waited for; matrix products, arithmetic and copies ran while one was open for 1% of the time, Pallas kernels for 0%

commit v1 on v0

v1 whole, which is shorter than its diff:
```python
import functools

import jax
import jax.numpy as jnp
from jax import lax
from jax.experimental import pallas as pl
from jax.experimental.pallas import tpu as pltpu
from jax.sharding import PartitionSpec as P

RIDGE = 1.0
DAMP = 0.5
MESH = pl.DeviceIdType.MESH
B = 128
VMEM_LIMIT = 62 * 1024 * 1024

CORE, XA, XB, YA, YB, ZH = range(6)
ORDERS = (
    (CORE, XA, XB, YA, YB, ZH),
    (CORE, YA, YB, XA, XB, ZH),
    (CORE, XB, XA, YB, YA, ZH),
    (CORE, YB, YA, XB, XA, ZH),
)
COLORS = len(ORDERS)
STAGES = 6


def place():
    r = lax.axis_index("row")
    core, y, x, z = lax.rem(r, 2), lax.rem(r // 2, 4), lax.rem(r // 8, 4), r // 32
    at = lambda z, x, y, core: ((z * 4 + x) * 4 + y) * 2 + core
    flip = lambda q: q + 1 - 2 * lax.rem(q, 2)
    bits = (core, lax.rem((x + 1) // 2, 2), x // 2, lax.rem((y + 1) // 2, 2), y // 2, z)
    partners = (
        at(z, x, y, 1 - core),
        at(z, flip(x), y, core),
        at(z, 3 - x, y, core),
        at(z, x, flip(y), core),
        at(z, x, 3 - y, core),
        at(1 - z, x, y, core),
    )
    return bits, partners


def meet(partners):
    barrier = pltpu.get_barrier_semaphore()
    for partner in partners:
        pl.semaphore_signal(barrier, inc=1, device_id={"row": partner}, device_id_type=MESH)
    pl.semaphore_wait(barrier, len(partners))


def send(src, dst, send_sem, recv_sem, partner):
    copy = pltpu.make_async_remote_copy(
        src_ref=src,
        dst_ref=dst,
        send_sem=send_sem,
        recv_sem=recv_sem,
        device_id={"row": partner},
        device_id_type=MESH,
    )
    copy.start()
    return copy


def packed_offsets(n):
    return [sum(n - B * i for i in range(j)) for j in range(n // B + 1)]


def packed_rows(n):
    return -(-packed_offsets(n)[-1] // 2048) * 2048


def gram_kernel(phi_ref, out_ref, phit, part, acc, land, rs_s, rs_r, ag_s, ag_r):
    bits, partners = place()
    n = phi_ref.shape[1]
    offsets = packed_offsets(n)
    total = out_ref.shape[0]
    for j in range(n // B):
        phit[B * j : B * j + B, :] = phi_ref[:, B * j : B * j + B].T
    for j in range(n // B):
        part[offsets[j] : offsets[j + 1], :] = lax.dot_general(
            phit[B * j :, :],
            phit[B * j : B * j + B, :],
            (((1,), (1,)), ((), ())),
            preferred_element_type=jnp.float32,
        )
    part[offsets[-1] :, :] = jnp.zeros((total - offsets[-1], B), jnp.float32)
    meet(partners)
    span = total // COLORS
    low = [jnp.int32(span * c) for c in range(COLORS)]

    def reduce_start(c, s, src):
        size = span >> (s + 1)
        axis = ORDERS[c][s]
        give = pl.multiple_of(low[c] + (1 - bits[axis]) * size, 8)
        low[c] = low[c] + bits[axis] * size
        base = span * c + (span - (span >> s))
        return send(
            src.at[pl.ds(give, size), :],
            land.at[pl.ds(base, size), :],
            rs_s.at[c, s],
            rs_r.at[c, s],
            partners[axis],
        )

    def gather_start(c, s):
        size = span >> (s + 1)
        axis = ORDERS[c][s]
        mine = pl.ds(pl.multiple_of(low[c], 8), size)
        low[c] = low[c] - bits[axis] * size
        return send(
            out_ref.at[mine, :], out_ref.at[mine, :], ag_s.at[c, s], ag_r.at[c, s], partners[axis]
        )

    pending = [reduce_start(c, 0, part) for c in range(COLORS)]
    for s in range(STAGES):
        size = span >> (s + 1)
        have = part if s == 0 else acc
        to = out_ref if s == STAGES - 1 else acc
        rows = min(size, 320)
        for c in range(COLORS):
            pending[c].wait()
            base = span * c + (span - (span >> s))
            here = low[c]

            @pl.loop(0, size // rows)
            def _(i):
                q = pl.ds(pl.multiple_of(here + i * rows, 8), rows)
                to[q, :] = have[q, :] + land[pl.ds(pl.multiple_of(base + i * rows, 8), rows), :]

            pending[c] = reduce_start(c, s + 1, acc) if s < STAGES - 1 else gather_start(c, s)
    for s in range(STAGES - 1, -1, -1):
        for c in range(COLORS):
            pending[c].wait()
            if s:
                pending[c] = gather_start(c, s - 1)


def gram_of_all_rows(phi):
    rows, n = phi.shape
    total = packed_rows(n)
    vmem = pl.BlockSpec(memory_space=pltpu.VMEM)
    return pl.pallas_call(
        gram_kernel,
        out_shape=jax.ShapeDtypeStruct((total, B), jnp.float32),
        in_specs=[vmem],
        out_specs=vmem,
        scratch_shapes=[pltpu.VMEM((n, rows), jnp.bfloat16)]
        + [pltpu.VMEM((total, B), jnp.float32)] * 3
        + [pltpu.SemaphoreType.DMA((COLORS, STAGES))] * 4,
        compiler_params=pltpu.CompilerParams(
            vmem_limit_bytes=VMEM_LIMIT, collective_id=0, has_side_effects=True
        ),
        cost_estimate=pl.CostEstimate(
            flops=2 * rows * n * n, bytes_accessed=150_000_000, transcendentals=0
        ),
        name="gram_of_all_rows",
    )(phi)


def split(v):
    high = v.astype(jnp.bfloat16)
    return high, (v - high.astype(jnp.float32)).astype(jnp.bfloat16)


def dot3(ah, al, bh, bl, dims):
    dot = functools.partial(
        lax.dot_general, dimension_numbers=(dims, ((), ())), preferred_element_type=jnp.float32
    )
    return dot(ah, bh) + (dot(ah, bl) + dot(al, bh))


def sweep8(strips):
    tile = (8, B)
    lane = lax.broadcasted_iota(jnp.int32, tile, 1)
    sub = lax.broadcasted_iota(jnp.int32, tile, 0)
    top = strips[0]
    row = lambda v, p: jnp.broadcast_to(v[p : p + 1, :], tile)
    column = lambda v, p: jnp.broadcast_to(v[:, p : p + 1], tile)
    key = lambda i, j: (i, j) if i >= j else (j, i)
    a = {}
    for q in range(8):
        col = column(top, q)
        for p in range(q, 8):
            a[p, q] = row(col, p)
    for p in range(8):
        inv = 1.0 / a[p, p]
        scaled = {i: a[key(i, p)] * inv for i in range(8) if i != p}
        for i in range(8):
            for j in range(i + 1):
                if i != p and j != p:
                    a[i, j] = a[i, j] - scaled[i] * a[key(j, p)]
        for i in scaled:
            a[key(i, p)] = scaled[i]
        a[p, p] = -inv
    held = jnp.where(lane < 8, jnp.where(lane == sub, -1.0, 0.0), top)
    rows = [row(held, q) for q in range(8)]
    swept = []
    for p in range(8):
        t = [a[key(p, q)] * rows[q] for q in range(8)]
        swept.append(((t[0] + t[1]) + (t[2] + t[3])) + ((t[4] + t[5]) + (t[6] + t[7])))
    out = []
    for v in strips[1:]:
        w = jnp.where(lane < 8, 0.0, v)
        for p in range(8):
            w = w + column(v, p) * swept[p]
        out.append(w)
    first = swept[0]
    for p in range(1, 8):
        first = jnp.where(sub == p, swept[p], first)
    out.append(-first)
    return tuple(pltpu.roll(v, B - 8, 1) for v in out)


def inverse(block):
    strips = tuple(block[8 * i : 8 * i + 8, :] for i in range(B // 8))
    strips = lax.fori_loop(0, B // 8, lambda _, held: sweep8(held), strips)
    return -jnp.concatenate(strips, axis=0)


def solve_kernel(
    gram_ref, phi_ref, res_ref, own_ref, out_ref, part, land, wh, wl, sh, sl, yh, yl, rs_s, rs_r, ag_s, ag_r
):
    bits, partners = place()
    n = phi_ref.shape[1]
    count = n // B
    offsets = packed_offsets(n)
    per = out_ref.shape[6]
    lanes = n // COLORS

    for i in range(2):
        for k in range(4):
            part[i, k // 2, k % 2] = lax.dot_general(
                res_ref[pl.ds((i * 4 + k) * 8 * per, 8 * per), :],
                phi_ref[...],
                (((1,), (0,)), ((), ())),
                preferred_element_type=jnp.float32,
            ).reshape(2, 2, 2, per, n)
    meet(partners)

    def index(c, s, value):
        where = [slice(None)] * STAGES
        for axis in ORDERS[c][:s]:
            where[axis] = bits[axis]
        where[ORDERS[c][s]] = value
        return tuple(where) + (slice(None), pl.ds(lanes * c, lanes))

    def reduce_start(c, s):
        axis = ORDERS[c][s]
        return send(
            part.at[index(c, s, 1 - bits[axis])],
            land.at[index(c, s, bits[axis])],
            rs_s.at[c, s],
            rs_r.at[c, s],
            partners[axis],
        )

    def reduce_add(c, s):
        axis = ORDERS[c][s]
        mine = index(c, s, bits[axis])
        theirs = index(c, s, 1 - bits[axis])
        part[mine] = part[mine] + land[theirs]

    def gather_start(c, s):
        mine = index(c, s, bits[ORDERS[c][s]])
        return send(
            out_ref.at[mine],
            out_ref.at[mine],
            ag_s.at[c, s],
            ag_r.at[c, s],
            partners[ORDERS[c][s]],
        )

    pending = [reduce_start(c, 0) for c in range(COLORS)]
    stage_before = {2: 0, 4: 1, 6: 2, 7: 3, 8: 4, 9: 5}

    eye = (
        lax.broadcasted_iota(jnp.int32, (B, B), 0) == lax.broadcasted_iota(jnp.int32, (B, B), 1)
    ).astype(jnp.float32)
    inverses = []
    for j in range(count):
        if j in stage_before:
            s = stage_before[j]
            for c in range(COLORS):
                pending[c].wait()
                reduce_add(c, s)
                if s < STAGES - 1:
                    pending[c] = reduce_start(c, s + 1)
        width = B * j
        start = B * j

        def updated(t):
            v = gram_ref[pl.ds(pl.multiple_of(offsets[j] - start + t * B, B), B), :]
            if j:
                at = pl.ds(pl.multiple_of(t * B, B), B)
                v = v - dot3(
                    wh[at, :width],
                    wl[at, :width],
                    sh[start : start + B, :width],
                    sl[start : start + B, :width],
                    ((1,), (1,)),
                )
            return v

        ih, il = split(inverse(updated(j) + RIDGE * eye))
        inverses.append((ih, il))
        wh[start : start + B, start : start + B] = ih
        wl[start : start + B, start : start + B] = il
        if j < count - 1:

            @pl.loop(j + 1, count)
            def _(t):
                at = pl.ds(pl.multiple_of(t * B, B), B)
                h, l = split(updated(t))
                sh[at, start : start + B] = h
                sl[at, start : start + B] = l
                h, l = split(dot3(h, l, ih, il, ((1,), (0,))))
                wh[at, start : start + B] = h
                wl[at, start : start + B] = l

    home = tuple(bits) + (slice(None), slice(None))
    rhs = part[home] - RIDGE * own_ref[...]
    for j in range(count):
        here = slice(B * j, B * j + B)
        y = rhs[:, here]
        if j:
            y = y - dot3(
                yh[:, : B * j], yl[:, : B * j], wh[here, : B * j], wl[here, : B * j], ((1,), (1,))
            )
        yh[:, here], yl[:, here] = split(y)
    for j in range(count - 1, -1, -1):
        here = slice(B * j, B * j + B)
        x = dot3(yh[:, here], yl[:, here], wh[here, here], wl[here, here], ((1,), (0,)))
        if j < count - 1:
            after = slice(B * j + B, n)
            x = x - dot3(yh[:, after], yl[:, after], wh[after, here], wl[after, here], ((1,), (0,)))
        out_ref[tuple(bits) + (slice(None), here)] = x
        yh[:, here], yl[:, here] = split(x)
    pending = [gather_start(c, STAGES - 1) for c in range(COLORS)]
    for s in range(STAGES - 1, -1, -1):
        for c in range(COLORS):
            pending[c].wait()
            if s:
                pending[c] = gather_start(c, s - 1)


def solution_of_all_classes(gram, phi, res, own):
    rows, n = phi.shape
    padded = res.shape[0]
    per = padded >> STAGES
    blocks = (2,) * STAGES + (per, n)
    vmem = pl.BlockSpec(memory_space=pltpu.VMEM)
    out = pl.pallas_call(
        solve_kernel,
        out_shape=jax.ShapeDtypeStruct(blocks, jnp.float32),
        in_specs=[vmem] * 4,
        out_specs=vmem,
        scratch_shapes=[pltpu.VMEM(blocks, jnp.float32)] * 2
        + [pltpu.VMEM((n, n), jnp.bfloat16)] * 4
        + [pltpu.VMEM((per, n), jnp.bfloat16)] * 2
        + [pltpu.SemaphoreType.DMA((COLORS, STAGES))] * 4,
        compiler_params=pltpu.CompilerParams(
            vmem_limit_bytes=VMEM_LIMIT, collective_id=1, has_side_effects=True
        ),
        cost_estimate=pl.CostEstimate(
            flops=2 * n * n * n, bytes_accessed=300_000_000, transcendentals=0
        ),
        name="solution_of_all_classes",
    )(gram, phi, res, own)
    return out.reshape(padded, n)


def body(inputs, labels, frequencies, phases, weights):
    groups = lax.axis_size("grp")
    width = frequencies.shape[1]
    classes = weights.shape[1]
    padded = -(-classes // 1024) * 1024
    scale = (2.0 / (groups * width)) ** 0.5
    swap = [(0, 1), (1, 0)]
    arg = (
        jnp.dot(inputs.astype(jnp.float32), frequencies, precision=lax.Precision.HIGHEST)
        + phases[None, :]
    )
    phi = (scale * jnp.cos(arg)).astype(jnp.bfloat16)
    onehot = (labels[:, None] == lax.broadcasted_iota(jnp.int32, (1, classes), 1)).astype(
        jnp.float32
    )
    own = jnp.dot(phi, weights.astype(jnp.bfloat16), preferred_element_type=jnp.float32)
    other = lax.ppermute(own, "grp", swap)
    gram = gram_of_all_rows(phi)
    residual = onehot - (own + other)
    res_low = jnp.pad(residual.astype(jnp.bfloat16).T, ((0, padded - classes), (0, 0)))

    bits, _ = place()
    piece = 0
    for bit in bits:
        piece = piece * 2 + bit
    per = padded // 64
    start = jnp.minimum(piece * per, classes - per)
    beyond = piece * per - start
    kept = lax.dynamic_slice(weights, (0, start), (width, per)).T
    own_weights = jnp.zeros_like(kept)
    for shift in sorted({max(0, p * per - (classes - per)) for p in range(64)}):
        if shift < per:
            moved = jnp.pad(kept[shift:, :], ((0, shift), (0, 0)))
            own_weights = jnp.where(beyond == shift, moved, own_weights)

    solution = solution_of_all_classes(gram, phi, res_low, own_weights)[:classes]
    step = DAMP * solution
    delta = lax.dot_general(
        phi, step.astype(jnp.bfloat16), (((1,), (1,)), ((), ())), preferred_element_type=jnp.float32
    )
    change = delta + lax.ppermute(delta, "grp", swap)
    return (weights + step.T, residual - change)


def solution(mesh):
    return jax.shard_map(
        body,
        mesh=mesh,
        in_specs=(P("row", None), P("row"), P(None, "grp"), P("grp"), P("grp", None)),
        out_specs=(P("grp", None), P("row", None)),
        check_vma=False,
    )
```

time: 1440 us -> 278 us (0.19)
  the two profiles are of different devices: /device:TPU:31 before, /device:TPU:10 now
where the time goes in v1:
time: 278 us; the launch traced here: 276 us
  Pallas kernels  222 us (80%)
  waiting for transfers between devices  17.5 us (6%)
  matrix products  17.1 us (6%)
  other arithmetic  12.9 us (5%)
  local copies, waits for them, and re-layouts  3.3 us (1%)
    pallas_call x1, Pallas kernels, solution_of_all_classes(): pl.pallas_call(solve_kernel, out_shape=jax.ShapeDtypeStruct(blocks, jnp.f...  154 us
    pallas_call x1, Pallas kernels, gram_of_all_rows(): pl.pallas_call(gram_kernel, out_shape=jax.ShapeDtypeStruct((total, B), jn...  67.7 us
    ppermute x1, waiting for transfers between devices, body(): change = delta + lax.ppermute(delta, 'grp', swap)  17.5 us
    dot_general x1, matrix products, body(): jnp.dot(inputs.astype(jnp.float32), frequencies, precision=lax.Precision....  8.24 us
    add x1, other arithmetic, body(): return (weights + step.T, residual - change)  6.79 us
  transfers between devices with their start and end apart: 2, of which 1 were waited for; matrix products, arithmetic and copies ran while one was open for 3% of the time, Pallas kernels for 25%

profile of v1, /device:TPU:10, one launch (start us, length us, event | category | flops | bytes accessed | tf_op | source)
XLA Modules:
  0.0 275.6 jit_solution(7309698520424683335)
XLA Ops:
  0.6 0.0 copy-start
  0.6 0.9 copy-done
  1.6 8.2 %fusion.8.phi_ref = bf16[256,1536]{1,0:T(8,128)(2,1)S(1)} fusion(bf16[256,512]{1,0:T(8,128)(2,1)S(1)} %copy-done, f32[512,1536]{1,0:T(8,128)} %param.7, f32[1536]{0:T(1024)} %param.8), kind=kOutput, calls=%fused_computation.10 | convolution fusion | flops 2417098752 | bytes 4200448 | tf_op jit(solution)/shard_map/dot_general | solution.py:380
  9.8 0.0 copy-start.2
  9.8 0.0 copy-start.4
  9.9 5.0 %fusion.4 = f32[256,1000]{0,1:T(8,128)} fusion(bf16[256,1536]{1,0:T(8,128)(2,1)S(1)} %fusion.8.phi_ref, f32[1536,1000]{0,1:T(8,128)} %param.9), kind=kOutput, calls=%fused_computation.5 | convolution fusion | flops 787968000 | bytes 7954432 | tf_op jit(solution)/shard_map/dot_general | solution.py:387
  14.8 1.9 collective-permute-start
  16.8 0.9 dynamic-slice_bitcast_fusion
  17.7 0.0 copy-done.2
  17.7 67.7 %gram_of_all_rows.1.gram_ref = f32[10240,128]{1,0:T(8,128)} custom-call(bf16[256,1536]{1,0:T(8,128)(2,1)} %copy-done.2), custom_call_target="tpu_custom_call" | custom-call | flops 1207959552 | bytes 150000000 | tf_op jit(solution)/shard_map/gram_of_all_rows/pallas_call | solution.py:142
  85.4 1.6 select_select_fusion.own_ref
  87.0 0.0 collective-permute-done
  87.0 0.0 copy-done.4
  87.0 1.7 convert_bitcast_fusion
  88.7 0.9 pad.8.res_ref
  89.6 0.0 copy-start.3
  89.6 154.3 %solution_of_all_classes.1 = f32[2,2,2,2,2,2,16,1536]{7,6,5,4,3,2,1,0:T(8,128)} custom-call(f32[10240,128]{1,0:T(8,128)} %gram_of_all_rows.1.gram_ref, bf16[256,1536]{1,0:T(8,128)(2,1)} %copy-done.2, bf16[1024,256]{1,0:T(8,128)(2,1)} %pad.8.res_ref, f32[16,1536]{1,0:T(8,128)} %select_select_fusion.own_ref), custom_call_target="tpu_custom_call" | custom-call | flops 7247757312 | bytes 300000000 | tf_op jit(solution)/shard_map/solution_of_all_classes/pallas_call | solution.py:352
  243.9 0.0 copy-start.1
  243.9 0.0 copy-done.3
  243.9 3.9 %fusion.1 = f32[256,1000]{0,1:T(8,128)S(1)} fusion(bf16[256,1536]{1,0:T(8,128)(2,1)S(1)} %copy-done.3, f32[1024,1536]{1,0:T(8,128)} %bitcast.13), kind=kOutput, calls=%fused_computation.3 | convolution fusion | flops 789504000 | bytes 7954432 | tf_op jit(solution)/shard_map/dot_general | solution.py:409
  247.8 0.1 collective-permute-start.1
  247.9 0.6 copy-done.1
  248.4 6.8 %bitcast_add_fusion = f32[1536,1000]{0,1:T(8,128)} fusion(f32[1536,1000]{0,1:T(8,128)} %param.9, f32[1024,1536]{1,0:T(8,128)S(1)} %bitcast.14), kind=kLoop, calls=%fused_computation.1 | loop fusion | flops 3072000 | bytes 18432000 | tf_op jit(solution)/shard_map/add | solution.py:413
  255.2 17.5 %collective-permute-done.1 = f32[256,1000]{0,1:T(8,128)S(1)} collective-permute-done((f32[256,1000]{0,1:T(8,128)S(1)}, f32[256,1000]{0,1:T(8,128)S(1)}, u32[]{:S(2)}, u32[]{:S(2)}) %collective-permute-start.1) | collective-permute-done | bytes 1024032 | tf_op jit(solution)/shard_map/ppermute | solution.py:412
  272.8 2.8 %add_subtract_fusion = f32[256,1000]{0,1:T(8,128)} fusion(f32[256,1000]{0,1:T(8,128)S(1)} %fusion.1, f32[256,1000]{0,1:T(8,128)S(1)} %collective-permute-done.1, f32[256,1000]{0,1:T(8,128)} %fusion.4, f32[256,1000]{0,1:T(8,128)} %collective-permute-done, s32[256]{0:T(256)S(1)} %copy-done.4), kind=kLoop, calls=%fused_computation.11 | loop fusion | flops 1536000 | bytes 5121024 | tf_op jit(solution)/shard_map/sub | solution.py:413
  (1 shorter events, 0.0 us)
Async XLA Ops:
  0.6 1.0 copy-start
  9.8 7.9 %copy-start.2 = (bf16[256,1536]{1,0:T(8,128)(2,1)}, bf16[256,1536]{1,0:T(8,128)(2,1)S(1)}, u32[]{:S(2)}) copy-start(bf16[256,1536]{1,0:T(8,128)(2,1)S(1)} %fusion.8.phi_ref) | copy-start | bytes 2359300
  9.8 77.1 %copy-start.4 = (s32[256]{0:T(256)S(1)}, s32[256]{0:T(256)}, u32[]{:S(2)}) copy-start(s32[256]{0:T(256)} %param.6) | copy-start | bytes 3076
  14.8 72.1 %collective-permute-start = (f32[256,1000]{0,1:T(8,128)}, f32[256,1000]{0,1:T(8,128)}, u32[]{:S(2)}, u32[]{:S(2)}) collective-permute-start(f32[256,1000]{0,1:T(8,128)} %fusion.4), channel_id=1, source_target_pairs={{0,64},{64,0},{1,65},{65,1},{2,66},{66,2},{3,67},{67,3},{4,68},{68... | collective-permute-start | bytes 3072008 | tf_op jit(solution)/shard_map/ppermute | solution.py:388
  89.6 154.3 %copy-start.3 = (bf16[256,1536]{1,0:T(8,128)(2,1)S(1)}, bf16[256,1536]{1,0:T(8,128)(2,1)}, u32[]{:S(2)}) copy-start(bf16[256,1536]{1,0:T(8,128)(2,1)} %copy-done.2) | copy-start | bytes 2359300
  243.9 4.6 %copy-start.1 = (f32[2,2,2,2,2,2,16,1536]{7,6,5,4,3,2,1,0:T(8,128)S(1)}, f32[2,2,2,2,2,2,16,1536]{7,6,5,4,3,2,1,0:T(8,128)}, u32[]{:S(2)}) copy-start(f32[2,2,2,2,2,2,16,1536]{7,6,5,4,3,2,1,0:T(8,128)} %solution_of_all_classes.1) | copy-start | bytes 18874372
  247.8 25.0 %collective-permute-start.1 = (f32[256,1000]{0,1:T(8,128)S(1)}, f32[256,1000]{0,1:T(8,128)S(1)}, u32[]{:S(2)}, u32[]{:S(2)}) collective-permute-start(f32[256,1000]{0,1:T(8,128)S(1)} %fusion.1), channel_id=1, source_target_pairs={{0,64},{64,0},{1,65},{65,1},{2,66},{66,2},{3,67},{67,3},{4,68},{68... | collective-permute-start | bytes 3072008 | tf_op jit(solution)/shard_map/ppermute | solution.py:412

commit v2 on v0

v2 whole, which is shorter than its diff:
```python
import functools

import jax
import jax.numpy as jnp
from jax import lax
from jax.experimental import pallas as pl
from jax.experimental.pallas import tpu as pltpu
from jax.sharding import PartitionSpec as P

RIDGE = 1.0
DAMP = 0.5
MESH = pl.DeviceIdType.MESH
B = 128
VMEM_LIMIT = 62 * 1024 * 1024

CORE, XA, XB, YA, YB, ZH = range(6)
ORDERS = (
    (CORE, XA, XB, YA, YB, ZH),
    (CORE, YA, YB, XA, XB, ZH),
    (CORE, XB, XA, YB, YA, ZH),
    (CORE, YB, YA, XB, XA, ZH),
)
COLORS = len(ORDERS)
STAGES = 6


def place():
    r = lax.axis_index("row")
    core, y, x, z = lax.rem(r, 2), lax.rem(r // 2, 4), lax.rem(r // 8, 4), r // 32
    at = lambda z, x, y, core: ((z * 4 + x) * 4 + y) * 2 + core
    flip = lambda q: q + 1 - 2 * lax.rem(q, 2)
    bits = (core, lax.rem((x + 1) // 2, 2), x // 2, lax.rem((y + 1) // 2, 2), y // 2, z)
    partners = (
        at(z, x, y, 1 - core),
        at(z, flip(x), y, core),
        at(z, 3 - x, y, core),
        at(z, x, flip(y), core),
        at(z, x, 3 - y, core),
        at(1 - z, x, y, core),
    )
    return bits, partners


def send(src, dst, send_sem, recv_sem, partner):
    copy = pltpu.make_async_remote_copy(
        src_ref=src,
        dst_ref=dst,
        send_sem=send_sem,
        recv_sem=recv_sem,
        device_id={"row": partner},
        device_id_type=MESH,
    )
    copy.start()
    return copy


def packed_offsets(n):
    return [sum(n - B * i for i in range(j)) for j in range(n // B + 1)]


def packed_rows(n):
    return -(-packed_offsets(n)[-1] // 2048) * 2048


def pieces(v):
    high = v.astype(jnp.bfloat16)
    rest = v - high.astype(jnp.float32)
    middle = rest.astype(jnp.bfloat16)
    return high, middle, (rest - middle.astype(jnp.float32)).astype(jnp.bfloat16)


def dot32(stack, right, dims):
    m = stack.shape[0] // 3
    dot = functools.partial(
        lax.dot_general, dimension_numbers=(dims, ((), ())), preferred_element_type=jnp.float32
    )
    high, middle, low = dot(stack, right[0]), dot(stack[: 2 * m], right[1]), dot(stack[:m], right[2])
    return high[:m] + ((high[m : 2 * m] + middle[:m]) + (high[2 * m :] + middle[m:] + low))


def stacked(v):
    return jnp.concatenate(pieces(v), axis=0)


def tree(t):
    return ((t[0] + t[1]) + (t[2] + t[3])) + ((t[4] + t[5]) + (t[6] + t[7]))


def key(i, j):
    return (i, j) if i >= j else (j, i)


def inverse8(a):
    for p in range(0, 8, 2):
        q = p + 1
        first, cross, second = a[p, p], a[q, p], a[q, q]
        det = first * second - cross * cross
        r = pl.reciprocal(det, approx=True)
        r = r * (2.0 - det * r)
        r = r * (2.0 - det * r)
        e, f, h = second * r, -(cross * r), first * r
        others = [i for i in range(8) if i not in (p, q)]
        u = {i: a[key(i, p)] for i in others}
        v = {i: a[key(i, q)] for i in others}
        mu = {i: u[i] * e + v[i] * f for i in others}
        mv = {i: u[i] * f + v[i] * h for i in others}
        for i in others:
            for j in others:
                if j <= i:
                    a[i, j] = a[i, j] - (mu[i] * u[j] + mv[i] * v[j])
        for i in others:
            a[key(i, p)], a[key(i, q)] = mu[i], mv[i]
        a[p, p], a[q, p], a[q, q] = -e, -f, -h
    return a


def inverse(block, scratch, parts):
    d_ref, p_ref, q_ref, t_ref, s_ref = scratch
    tile = (8, B)
    lane = lax.broadcasted_iota(jnp.int32, tile, 1)
    sub = lax.broadcasted_iota(jnp.int32, tile, 0)
    lanes = lax.broadcasted_iota(jnp.int32, (B, B), 1)
    d_ref[...] = block
    p_ref[...] = jnp.zeros(p_ref.shape, p_ref.dtype)
    q_ref[...] = jnp.zeros(q_ref.shape, q_ref.dtype)
    t_ref[...] = jnp.zeros(tile, jnp.float32)

    def columns(v, k):
        return [
            jnp.take_along_axis(v, jnp.full(tile, k + q, jnp.int32), axis=1) for q in range(8)
        ]

    def late():
        return lax.dot_general(
            p_ref[...], q_ref[...], (((0,), (0,)), ((), ())), preferred_element_type=jnp.float32
        )

    def step(b, top, also):
        k = pl.multiple_of(b * 8, 8)
        was = pl.multiple_of(lax.rem(k + B - 8, B), 8)
        update = late()
        below = d_ref[pl.ds(pl.multiple_of(lax.rem(k + 8, B), 8), 8), :]
        before = jnp.logical_and(jnp.logical_and(lane >= was, lane < was + 8), k > 0)
        cols = columns(below, was)
        below = jnp.where(before, 0.0, below) + tree(
            [cols[p] * jnp.broadcast_to(t_ref[p : p + 1, :], tile) for p in range(8)]
        )
        for q, col in enumerate(columns(top, k)):
            s_ref[8 * q : 8 * q + 8, :] = col
        a = {}
        for q in range(8):
            for p in range(q, 8):
                a[p, q] = jnp.broadcast_to(s_ref[8 * q + p : 8 * q + p + 1, :], tile)
        a = inverse8(a)
        now = jnp.logical_and(lane >= k, lane < k + 8)
        s_ref[64:72, :] = jnp.where(now, jnp.where(lane - k == sub, -1.0, 0.0), top)
        rows = [jnp.broadcast_to(s_ref[64 + q : 65 + q, :], tile) for q in range(8)]
        swept = [tree([a[key(p, q)] * rows[q] for q in range(8)]) for p in range(8)]
        cols = columns(below, k)
        below = jnp.where(now, 0.0, below) + tree([cols[p] * swept[p] for p in range(8)])
        strip = swept[0]
        for p in range(1, 8):
            strip = jnp.where(sub == p, swept[p], strip)
        place = lanes - was
        done = jnp.logical_and(k > 0, jnp.logical_and(place >= 0, place < 8))
        d_ref[...] = jnp.where(done, 0.0, d_ref[...]) + update
        d_ref[pl.ds(was, 8), :] = jnp.where(k > 0, -t_ref[...], d_ref[pl.ds(was, 8), :])
        uh, um, ul = (v.astype(jnp.float32) for v in pieces(top))
        th, tm, tl = (v.astype(jnp.float32) for v in pieces(strip))
        p_ref[...] = jnp.concatenate([uh, uh, um, uh, um, ul], axis=0).astype(jnp.bfloat16)
        q_ref[...] = jnp.concatenate([th, tm, th, tl, tm, th], axis=0).astype(jnp.bfloat16)
        t_ref[...] = strip
        if also is not None:
            also(b)
        return below

    top = block[:8, :]
    begin = 0
    for steps, also, after in parts:
        if steps:
            top = lax.fori_loop(
                begin, begin + steps, lambda b, v, also=also: step(b, v, also), top
            )
        begin += steps
        after()
    d = jnp.where(lanes >= B - 8, 0.0, d_ref[...]) + late()
    return -jnp.concatenate([d[: B - 8, :], -t_ref[...]], axis=0)


def sweep_kernel(
    phi_ref, own_ref, label_ref, weight_ref,
    out_ref, res_ref,
    phit, gpart, gland, a_ref, rpart, rland, other, low_ref, lowt, w_ref, rs, dv, ys,
    d_ref, p_ref, q_ref, t_ref, s_ref,
    swap_sem, grs_s, grs_r, gag_s, gag_r, rs_s, rs_r, ag_s, ag_r,
):
    bits, partners = place()
    group = lax.axis_index("grp")
    n = phi_ref.shape[1]
    count = n // B
    offsets = packed_offsets(n)
    total = a_ref.shape[0]
    classes = own_ref.shape[1]
    per = out_ref.shape[6]
    lanes = n // COLORS
    block = lambda j: slice(B * j, B * j + B)

    for j in range(count):
        phit[block(j), :] = phi_ref[:, block(j)].T
    for j in range(count):
        gpart[offsets[j] : offsets[j + 1], :] = lax.dot_general(
            phit[B * j :, :],
            phit[block(j), :],
            (((1,), (1,)), ((), ())),
            preferred_element_type=jnp.float32,
        )
    gpart[offsets[-1] :, :] = jnp.zeros((total - offsets[-1], B), jnp.float32)

    barrier = pltpu.get_barrier_semaphore()
    pl.semaphore_signal(barrier, inc=1, device_id={"grp": 1 - group}, device_id_type=MESH)
    for partner in partners:
        pl.semaphore_signal(barrier, inc=1, device_id={"row": partner}, device_id_type=MESH)
    pl.semaphore_wait(barrier, len(partners) + 1)

    swap = pltpu.make_async_remote_copy(
        src_ref=own_ref,
        dst_ref=other,
        send_sem=swap_sem.at[0],
        recv_sem=swap_sem.at[1],
        device_id={"grp": 1 - group},
        device_id_type=MESH,
    )
    swap.start()

    def gram_wave(w, base, rows):
        span = rows // COLORS
        low = [jnp.int32(base + span * c) for c in range(COLORS)]

        def reduce_start(c, s, src):
            size = span >> (s + 1)
            axis = ORDERS[c][s]
            give = pl.multiple_of(low[c] + (1 - bits[axis]) * size, 8)
            low[c] = low[c] + bits[axis] * size
            land = base + span * c + (span - (span >> s))
            return send(
                src.at[pl.ds(give, size), :],
                gland.at[pl.ds(land, size), :],
                grs_s.at[w, c, s],
                grs_r.at[w, c, s],
                partners[axis],
            )

        def gather_start(c, s):
            size = span >> (s + 1)
            axis = ORDERS[c][s]
            mine = pl.ds(pl.multiple_of(low[c], 8), size)
            low[c] = low[c] - bits[axis] * size
            return send(
                a_ref.at[mine, :], a_ref.at[mine, :], gag_s.at[w, c, s], gag_r.at[w, c, s], partners[axis]
            )

        pending = [reduce_start(c, 0, gpart) for c in range(COLORS)]
        yield
        for s in range(STAGES):
            size = span >> (s + 1)
            to = a_ref if s == STAGES - 1 else gpart
            step = min(size, 256)
            for c in range(COLORS):
                pending[c].wait()
                land = base + span * c + (span - (span >> s))
                here = low[c]

                @pl.loop(0, size // step)
                def _(i):
                    q = pl.ds(pl.multiple_of(here + i * step, 8), step)
                    to[q, :] = gpart[q, :] + gland[pl.ds(pl.multiple_of(land + i * step, 8), step), :]

                pending[c] = reduce_start(c, s + 1, gpart) if s < STAGES - 1 else gather_start(c, s)
            yield
        for s in range(STAGES - 1, -1, -1):
            for c in range(COLORS):
                pending[c].wait()
                if s:
                    pending[c] = gather_start(c, s - 1)
            yield

    def index(c, s, value):
        where = [slice(None)] * STAGES
        for axis in ORDERS[c][:s]:
            where[axis] = bits[axis]
        where[ORDERS[c][s]] = value
        return tuple(where) + (slice(None), pl.ds(lanes * c, lanes))

    def rhs_sum():
        swap.wait()
        hot = label_ref[...] == lax.broadcasted_iota(jnp.int32, (1, classes), 1)
        residual = hot.astype(jnp.float32) - (own_ref[...] + other[...])
        res_ref[...] = residual
        low_ref[...] = jnp.zeros(low_ref.shape, low_ref.dtype)
        low_ref[:, :classes] = residual.astype(jnp.bfloat16)
        for i in range(lowt.shape[0] // B):
            lowt[block(i), :] = low_ref[:, block(i)].T
        for i in range(8):
            rpart[i // 4, i // 2 % 2, i % 2] = lax.dot_general(
                lowt[i * 8 * per : (i + 1) * 8 * per, :],
                phi_ref[...],
                (((1,), (0,)), ((), ())),
                preferred_element_type=jnp.float32,
            ).reshape(2, 2, 2, per, n)

        def start(c, s):
            axis = ORDERS[c][s]
            return send(
                rpart.at[index(c, s, 1 - bits[axis])],
                rland.at[index(c, s, bits[axis])],
                rs_s.at[c, s],
                rs_r.at[c, s],
                partners[axis],
            )

        pending = [start(c, 0) for c in range(COLORS)]
        yield
        for s in range(STAGES):
            for c in range(COLORS):
                pending[c].wait()
                mine = index(c, s, bits[ORDERS[c][s]])
                rpart[mine] = rpart[mine] + rland[index(c, s, 1 - bits[ORDERS[c][s]])]
                if s < STAGES - 1:
                    pending[c] = start(c, s + 1)
            yield

    waves = dict(
        A=gram_wave(0, 0, 2048),
        B=gram_wave(1, 2048, 4096),
        C=gram_wave(2, 6144, total - 6144),
        R=rhs_sum(),
    )

    def go(names):
        for name in names:
            next(waves[name], None)

    hooks = dict(HOOKS)

    scratch = (d_ref, p_ref, q_ref, t_ref, s_ref)
    eye = (
        lax.broadcasted_iota(jnp.int32, (B, B), 0) == lax.broadcasted_iota(jnp.int32, (B, B), 1)
    ).astype(jnp.float32)
    go(hooks["start"])
    system = a_ref[:B, :] + RIDGE * eye
    for j in range(count):
        go(hooks.get((j, 0), ""))
        here = block(j)
        width = B * j

        def row_of(t, j=j, here=here, width=width):
            at = pl.ds(pl.multiple_of(t * B, B), B)
            old = pl.ds(pl.multiple_of(offsets[j - 1] + (t - j + 1) * B, B), B)
            new = pl.ds(pl.multiple_of(offsets[j] + (t - j) * B, B), B)
            w_ref[at, block(j - 1)] = dot32(
                stacked(a_ref[old, :]), (dv[0], dv[1], dv[2]), ((1,), (0,))
            )
            a_ref[new, :] = a_ref[new, :] - dot32(
                stacked(w_ref[at, :width]), [rs[i, :, :width] for i in range(3)], ((1,), (1,))
            )

        with_rows = count - 1 - j if j else 0
        parts = [
            (with_rows, lambda b, j=j, f=row_of: f(j + 1 + b), lambda j=j: go(hooks.get((j, 1), ""))),
            (B // 8 - with_rows, None, lambda j=j: go(hooks.get((j, 2), ""))),
        ]
        inv = inverse(system, scratch, parts)
        w_ref[here, here] = inv
        if j < count - 1:
            dv[0], dv[1], dv[2] = pieces(inv)
            after = block(j + 1)
            w_ref[after, here] = dot32(
                stacked(a_ref[offsets[j] + B : offsets[j] + 2 * B, :]),
                (dv[0], dv[1], dv[2]),
                ((1,), (0,)),
            )
            for k in range(j + 1):
                at = offsets[k] + (j + 1 - k) * B
                rs[0, :, block(k)], rs[1, :, block(k)], rs[2, :, block(k)] = pieces(
                    a_ref[at : at + B, :]
                )
            width = B * (j + 1)
            system = (a_ref[offsets[j + 1] : offsets[j + 1] + B, :] + RIDGE * eye) - dot32(
                stacked(w_ref[after, :width]), [rs[i, :, :width] for i in range(3)], ((1,), (1,))
            )

    rhs = rpart[tuple(bits)] - RIDGE * weight_ref[...]
    for j in range(count):
        here = block(j)
        y = rhs[:, here]
        if j:
            y = y - dot32(ys[:, : B * j], pieces(w_ref[here, : B * j]), ((1,), (1,)))
        ys[:, here] = stacked(y)

    def gather(c):
        def start(s):
            mine = index(c, s, bits[ORDERS[c][s]])
            return send(
                out_ref.at[mine], out_ref.at[mine], ag_s.at[c, s], ag_r.at[c, s], partners[ORDERS[c][s]]
            )

        copy = start(STAGES - 1)
        for s in range(STAGES - 1, -1, -1):
            yield
            copy.wait()
            if s:
                copy = start(s - 1)

    gathers = []
    for j in range(count - 1, -1, -1):
        here = block(j)
        x = dot32(ys[:, here], pieces(w_ref[here, here]), ((1,), (0,)))
        if j < count - 1:
            after = slice(B * j + B, n)
            x = x - dot32(ys[:, after], pieces(w_ref[after, here]), ((1,), (0,)))
        out_ref[tuple(bits) + (slice(None), here)] = x
        ys[:, here] = stacked(x)
        if B * j % lanes == 0:
            for held in gathers:
                next(held, None)
            gathers.append(gather(B * j // lanes))
            next(gathers[-1])
    for _ in range(STAGES):
        for held in gathers:
            next(held, None)


HOOKS = (
    ("start", "ABC" + "AABAABCAABABCAABACABA"),
    ((0, 0), "BC"),
    ((0, 1), "BC"),
    ((0, 2), "BCBCBBB"),
    ((1, 0), "C"),
    ((1, 1), "C"),
    ((2, 0), "C"),
    ((2, 1), "C"),
    ((3, 0), "CC"),
    ((3, 2), "CCCCCR"),
    ((5, 0), "R"),
    ((6, 0), "R"),
    ((7, 0), "R"),
    ((8, 0), "R"),
    ((9, 0), "R"),
    ((10, 0), "RR"),
)


def sweep_over_all_rows(phi, own, labels, own_weights, padded):
    rows, n = phi.shape
    classes = own.shape[1]
    total = packed_rows(n)
    per = padded >> STAGES
    blocks = (2,) * STAGES + (per, n)
    vmem = pl.BlockSpec(memory_space=pltpu.VMEM)
    sem = pltpu.SemaphoreType.DMA
    f32, bf16 = jnp.float32, jnp.bfloat16
    solution, residual = pl.pallas_call(
        sweep_kernel,
        out_shape=(
            jax.ShapeDtypeStruct(blocks, f32),
            jax.ShapeDtypeStruct((rows, classes), f32),
        ),
        in_specs=[vmem] * 4,
        out_specs=(vmem, vmem),
        scratch_shapes=[
            pltpu.VMEM((n, rows), bf16),
            pltpu.VMEM((total, B), f32),
            pltpu.VMEM((total, B), f32),
            pltpu.VMEM((total, B), f32),
            pltpu.VMEM(blocks, f32),
            pltpu.VMEM(blocks, f32),
            pltpu.VMEM((rows, classes), f32),
            pltpu.VMEM((rows, padded), bf16),
            pltpu.VMEM((padded, rows), bf16),
            pltpu.VMEM((n, n), f32),
            pltpu.VMEM((3, B, n), bf16),
            pltpu.VMEM((3, B, B), bf16),
            pltpu.VMEM((3 * per, n), bf16),
            pltpu.VMEM((B, B), f32),
            pltpu.VMEM((48, B), bf16),
            pltpu.VMEM((48, B), bf16),
            pltpu.VMEM((8, B), f32),
            pltpu.VMEM((72, B), f32),
            sem((2,)),
            *[sem((3, COLORS, STAGES))] * 4,
            *[sem((COLORS, STAGES))] * 4,
        ],
        compiler_params=pltpu.CompilerParams(
            vmem_limit_bytes=VMEM_LIMIT, collective_id=0, has_side_effects=True
        ),
        cost_estimate=pl.CostEstimate(
            flops=2 * n * n * n, bytes_accessed=300_000_000, transcendentals=0
        ),
        name="sweep_over_all_rows",
    )(phi, own, labels.reshape(rows, 1), own_weights)
    return solution.reshape(padded, n), residual


def body(inputs, labels, frequencies, phases, weights):
    groups = lax.axis_size("grp")
    width = frequencies.shape[1]
    classes = weights.shape[1]
    padded = -(-classes // 1024) * 1024
    scale = (2.0 / (groups * width)) ** 0.5
    swap = [(0, 1), (1, 0)]
    arg = (
        jnp.dot(inputs.astype(jnp.float32), frequencies, precision=lax.Precision.HIGHEST)
        + phases[None, :]
    )
    phi = (scale * jnp.cos(arg)).astype(jnp.bfloat16)
    own = jnp.dot(phi, weights.astype(jnp.bfloat16), preferred_element_type=jnp.float32)
    bits, _ = place()
    piece = 0
    for bit in bits:
        piece = piece * 2 + bit
    per = padded // 64
    start = jnp.minimum(piece * per, classes - per)
    beyond = piece * per - start
    kept = lax.dynamic_slice(weights, (0, start), (width, per)).T
    own_weights = jnp.zeros_like(kept)
    for shift in sorted({max(0, p * per - (classes - per)) for p in range(64)}):
        if shift < per:
            moved = jnp.pad(kept[shift:, :], ((0, shift), (0, 0)))
            own_weights = jnp.where(beyond == shift, moved, own_weights)

    solution, residual = sweep_over_all_rows(phi, own, labels, own_weights, padded)
    solution = solution[:classes]
    step = DAMP * solution
    delta = lax.dot_general(
        phi, step.astype(jnp.bfloat16), (((1,), (1,)), ((), ())), preferred_element_type=jnp.float32
    )
    change = delta + lax.ppermute(delta, "grp", swap)
    return (weights + step.T, residual - change)


def solution(mesh):
    return jax.shard_map(
        body,
        mesh=mesh,
        in_specs=(P("row", None), P("row"), P(None, "grp"), P("grp"), P("grp", None)),
        out_specs=(P("grp", None), P("row", None)),
        check_vma=False,
    )
```

time: 1440 us -> 263 us (0.18)
  the two profiles are of different devices: /device:TPU:31 before, /device:TPU:10 now
where the time goes in v2:
time: 263 us; the launch traced here: 261 us
  Pallas kernels  212 us (81%)
  matrix products  17.3 us (7%)
  waiting for transfers between devices  15.3 us (6%)
  other arithmetic  11.7 us (4%)
  local copies, waits for them, and re-layouts  3.7 us (1%)
    pallas_call x1, Pallas kernels, sweep_over_all_rows(): pl.pallas_call(sweep_kernel, out_shape=(jax.ShapeDtypeStruct(blocks, f32)...  212 us
    ppermute x1, waiting for transfers between devices, body(): change = delta + lax.ppermute(delta, 'grp', swap)  15.3 us
    add x1, other arithmetic, body(): return (weights + step.T, residual - change)  8.61 us
    dot_general x1, matrix products, body(): jnp.dot(inputs.astype(jnp.float32), frequencies, precision=lax.Precision....  8.26 us
  transfers between devices with their start and end apart: 1, of which 1 were waited for; matrix products, arithmetic and copies ran while one was open for 3% of the time, Pallas kernels for 0%

profile of v2, /device:TPU:10, one launch (start us, length us, event | category | flops | bytes accessed | tf_op | source)
XLA Modules:
  0.0 261.5 jit_solution(8206407507931573075)
XLA Ops:
  0.6 0.0 copy-start
  0.8 0.9 dynamic-slice_bitcast_fusion
  1.7 0.0 copy-start.2
  1.8 0.0 copy-done
  1.8 8.3 %fusion.8.phi_ref = bf16[256,1536]{1,0:T(8,128)(2,1)S(1)} fusion(bf16[256,512]{1,0:T(8,128)(2,1)S(1)} %copy-done, f32[512,1536]{1,0:T(8,128)} %param.7, f32[1536]{0:T(1024)} %param.8), kind=kOutput, calls=%fused_computation.10 | convolution fusion | flops 2417098752 | bytes 4200448 | tf_op jit(solution)/shard_map/dot_general | solution.py:512
  10.0 0.0 copy-start.1
  10.0 5.0 %fusion.4.own_ref = f32[256,1000]{1,0:T(8,128)} fusion(bf16[256,1536]{1,0:T(8,128)(2,1)S(1)} %fusion.8.phi_ref, f32[1536,1000]{0,1:T(8,128)} %param.9), kind=kOutput, calls=%fused_computation.5 | convolution fusion | flops 787968000 | bytes 7954432 | tf_op jit(solution)/shard_map/dot_general | solution.py:516
  15.1 0.0 copy-done.2
  15.1 0.8 copy.17.label_ref
  15.9 1.6 select_select_fusion.weight_ref
  17.4 0.0 copy-done.1
  17.4 211.9 %sweep_over_all_rows.1 = (f32[2,2,2,2,2,2,16,1536]{7,6,5,4,3,2,1,0:T(8,128)}, f32[256,1000]{1,0:T(8,128)}) custom-call(bf16[256,1536]{1,0:T(8,128)(2,1)} %copy-done.1, f32[256,1000]{1,0:T(8,128)} %fusion.4.own_ref, s32[256,1]{1,0:T(8,128)} %copy.17.label_ref, f32[16,1536]{1,0:T(8,128)} %select_select_fusion.weight_ref), custom_call_target="tpu_custom_call" | custom-call | flops 7247757312 | bytes 300000000 | tf_op jit(solution)/shard_map/sweep_over_all_rows/pallas_call | solution.py:462
  229.4 4.0 %fusion.1 = f32[256,1000]{0,1:T(8,128)S(1)} fusion(bf16[256,1536]{1,0:T(8,128)(2,1)} %copy-done.1, f32[1024,1536]{1,0:T(8,128)} %bitcast.12), kind=kOutput, calls=%fused_computation.3 | convolution fusion | flops 789504000 | bytes 7954432 | tf_op jit(solution)/shard_map/dot_general | solution.py:534
  233.4 0.7 collective-permute-start
  234.1 0.3 copy.18
  234.4 8.6 %bitcast_add_fusion = f32[1536,1000]{0,1:T(8,128)} fusion(f32[1536,1000]{0,1:T(8,128)} %param.9, f32[1024,1536]{1,0:T(8,128)} %bitcast.13), kind=kLoop, calls=%fused_computation.1 | loop fusion | flops 3072000 | bytes 18432000 | tf_op jit(solution)/shard_map/add | solution.py:538
  243.0 15.3 %collective-permute-done = f32[256,1000]{0,1:T(8,128)S(1)} collective-permute-done((f32[256,1000]{0,1:T(8,128)S(1)}, f32[256,1000]{0,1:T(8,128)S(1)}, u32[]{:S(2)}, u32[]{:S(2)}) %collective-permute-start) | collective-permute-done | bytes 1024032 | tf_op jit(solution)/shard_map/ppermute | solution.py:537
  258.4 0.3 copy.19
  258.7 1.5 add_subtract_fusion
  260.2 1.3 copy.20
  (1 shorter events, 0.0 us)
Async XLA Ops:
  0.6 1.1 copy-start
  1.7 13.3 %copy-start.2 = (s32[256]{0:T(256)S(1)}, s32[256]{0:T(256)}, u32[]{:S(2)}) copy-start(s32[256]{0:T(256)} %param.6) | copy-start | bytes 3076
  10.0 7.4 %copy-start.1 = (bf16[256,1536]{1,0:T(8,128)(2,1)}, bf16[256,1536]{1,0:T(8,128)(2,1)S(1)}, u32[]{:S(2)}) copy-start(bf16[256,1536]{1,0:T(8,128)(2,1)S(1)} %fusion.8.phi_ref) | copy-start | bytes 2359300
  233.4 25.0 %collective-permute-start = (f32[256,1000]{0,1:T(8,128)S(1)}, f32[256,1000]{0,1:T(8,128)S(1)}, u32[]{:S(2)}, u32[]{:S(2)}) collective-permute-start(f32[256,1000]{0,1:T(8,128)S(1)} %fusion.1), channel_id=1, source_target_pairs={{0,64},{64,0},{1,65},{65,1},{2,66},{66,2},{3,67},{67,3},{4,68},{68... | collective-permute-start | bytes 3072008 | tf_op jit(solution)/shard_map/ppermute | solution.py:537

commit v3 on v2

--- a/solution.py
+++ b/solution.py
@@ -188,11 +188,11 @@
 
 
 def sweep_kernel(
-    phi_ref, own_ref, label_ref, weight_ref,
-    out_ref, res_ref,
-    phit, gpart, gland, a_ref, rpart, rland, other, low_ref, lowt, w_ref, rs, dv, ys,
+    phi_ref, all_ref, label_ref,
+    out_ref, res_ref, delta_ref,
+    phit, gpart, gland, a_ref, rpart, rland, held_ref, own_ref, other, early, late_ref, low_ref, lowt, w_ref, rs, dv, ys,
     d_ref, p_ref, q_ref, t_ref, s_ref,
-    swap_sem, grs_s, grs_r, gag_s, gag_r, rs_s, rs_r, ag_s, ag_r,
+    swap_sem, copy_sem, grs_s, grs_r, gag_s, gag_r, rs_s, rs_r, ag_s, ag_r,
 ):
     bits, partners = place()
     group = lax.axis_index("grp")
@@ -200,11 +200,15 @@
     count = n // B
     offsets = packed_offsets(n)
     total = a_ref.shape[0]
-    classes = own_ref.shape[1]
-    per = out_ref.shape[6]
+    classes = all_ref.shape[0]
+    per = out_ref.shape[-2]
+    half = lowt.shape[0] // 2
     lanes = n // COLORS
     block = lambda j: slice(B * j, B * j + B)
 
+    bring = pltpu.make_async_copy(all_ref, held_ref.at[pl.ds(0, classes), :], copy_sem)
+    bring.start()
+    held_ref[classes:, :] = jnp.zeros((held_ref.shape[0] - classes, n), jnp.float32)
     for j in range(count):
         phit[block(j), :] = phi_ref[:, block(j)].T
     for j in range(count):
@@ -230,7 +234,19 @@
         device_id={"grp": 1 - group},
         device_id_type=MESH,
     )
-    swap.start()
+
+    def own_prediction():
+        bring.wait()
+        for at in range(0, classes, B):
+            cols = slice(at, min(at + B, classes))
+            own_ref[:, cols] = lax.dot_general(
+                phi_ref[...],
+                held_ref[cols, :].astype(jnp.bfloat16),
+                (((1,), (1,)), ((), ())),
+                preferred_element_type=jnp.float32,
+            )
+        swap.start()
+        yield
 
     def gram_wave(w, base, rows):
         span = rows // COLORS
@@ -284,29 +300,34 @@
                     pending[c] = gather_start(c, s - 1)
             yield
 
-    def index(c, s, value):
+    def index(c, s, value, h=slice(None)):
         where = [slice(None)] * STAGES
         for axis in ORDERS[c][:s]:
             where[axis] = bits[axis]
         where[ORDERS[c][s]] = value
-        return tuple(where) + (slice(None), pl.ds(lanes * c, lanes))
+        return (h,) + tuple(where) + (slice(None), pl.ds(lanes * c, lanes))
 
     def rhs_sum():
         swap.wait()
-        hot = label_ref[...] == lax.broadcasted_iota(jnp.int32, (1, classes), 1)
-        residual = hot.astype(jnp.float32) - (own_ref[...] + other[...])
-        res_ref[...] = residual
         low_ref[...] = jnp.zeros(low_ref.shape, low_ref.dtype)
-        low_ref[:, :classes] = residual.astype(jnp.bfloat16)
+        for i in range(phi_ref.shape[0] // B):
+            label = jnp.broadcast_to(label_ref[:, block(i)], (B, B)).T
+            for at in range(0, classes, B):
+                cols = slice(at, min(at + B, classes))
+                wide = cols.stop - cols.start
+                hot = label[:, :wide] == at + lax.broadcasted_iota(jnp.int32, (B, wide), 1)
+                residual = hot.astype(jnp.float32) - (own_ref[block(i), cols] + other[block(i), cols])
+                res_ref[block(i), cols] = residual
+                low_ref[block(i), cols] = residual.astype(jnp.bfloat16)
         for i in range(lowt.shape[0] // B):
             lowt[block(i), :] = low_ref[:, block(i)].T
         for i in range(8):
             rpart[i // 4, i // 2 % 2, i % 2] = lax.dot_general(
-                lowt[i * 8 * per : (i + 1) * 8 * per, :],
+                lowt[i * 16 * per : (i + 1) * 16 * per, :],
                 phi_ref[...],
                 (((1,), (0,)), ((), ())),
                 preferred_element_type=jnp.float32,
-            ).reshape(2, 2, 2, per, n)
+            ).reshape(2, 2, 2, 2, per, n)
 
         def start(c, s):
             axis = ORDERS[c][s]
@@ -333,6 +354,7 @@
         A=gram_wave(0, 0, 2048),
         B=gram_wave(1, 2048, 4096),
         C=gram_wave(2, 6144, total - 6144),
+        O=own_prediction(),
         R=rhs_sum(),
     )
 
@@ -389,7 +411,14 @@
                 stacked(w_ref[after, :width]), [rs[i, :, :width] for i in range(3)], ((1,), (1,))
             )
 
-    rhs = rpart[tuple(bits)] - RIDGE * weight_ref[...]
+    mine = (slice(None),) + tuple(bits)
+    piece = 0
+    for bit in bits:
+        piece = piece * 2 + bit
+    weights = [
+        held_ref[pl.ds(pl.multiple_of(h * half + piece * per, per), per), :] for h in range(2)
+    ]
+    rhs = rpart[mine].reshape(2 * per, n) - RIDGE * jnp.concatenate(weights, axis=0)
     for j in range(count):
         here = block(j)
         y = rhs[:, here]
@@ -397,11 +426,15 @@
             y = y - dot32(ys[:, : B * j], pieces(w_ref[here, : B * j]), ((1,), (1,)))
         ys[:, here] = stacked(y)
 
-    def gather(c):
+    def gather(c, h):
         def start(s):
-            mine = index(c, s, bits[ORDERS[c][s]])
+            at = index(c, s, bits[ORDERS[c][s]], h)
             return send(
-                out_ref.at[mine], out_ref.at[mine], ag_s.at[c, s], ag_r.at[c, s], partners[ORDERS[c][s]]
+                out_ref.at[at],
+                out_ref.at[at],
+                ag_s.at[h, c, s],
+                ag_r.at[h, c, s],
+                partners[ORDERS[c][s]],
             )
 
         copy = start(STAGES - 1)
@@ -411,62 +444,86 @@
             if s:
                 copy = start(s - 1)
 
-    gathers = []
+    gathers = ([], [])
     for j in range(count - 1, -1, -1):
         here = block(j)
         x = dot32(ys[:, here], pieces(w_ref[here, here]), ((1,), (0,)))
         if j < count - 1:
             after = slice(B * j + B, n)
             x = x - dot32(ys[:, after], pieces(w_ref[after, here]), ((1,), (0,)))
-        out_ref[tuple(bits) + (slice(None), here)] = x
+        out_ref[mine + (slice(None), here)] = x.reshape(2, per, B)
         ys[:, here] = stacked(x)
         if B * j % lanes == 0:
-            for held in gathers:
+            for held in gathers[0]:
                 next(held, None)
-            gathers.append(gather(B * j // lanes))
-            next(gathers[-1])
-    for _ in range(STAGES):
-        for held in gathers:
+            gathers[0].append(gather(B * j // lanes, 0))
+            next(gathers[0][-1])
+    for r in range(STAGES):
+        for held in gathers[0]:
             next(held, None)
+        if r == 0:
+            gathers[1].extend(gather(c, 1) for c in range(COLORS - 1, -1, -1))
+        for held in gathers[1]:
+            next(held, None)
+    def predictions(h, i):
+        return lax.dot_general(
+            phi_ref[...],
+            (DAMP * out_ref[h, i // 2, i % 2].reshape(16 * per, n)).astype(jnp.bfloat16),
+            (((1,), (1,)), ((), ())),
+            preferred_element_type=jnp.float32,
+        )
+
+    for i in range(4):
+        early[:, i * 16 * per : (i + 1) * 16 * per] = predictions(0, i)
+    change = pltpu.make_async_remote_copy(
+        src_ref=early,
+        dst_ref=late_ref,
+        send_sem=swap_sem.at[2],
+        recv_sem=swap_sem.at[3],
+        device_id={"grp": 1 - group},
+        device_id_type=MESH,
+    )
+    change.start()
+    for held in gathers[1]:
+        next(held, None)
+    for i in range(4):
+        at = i * 16 * per
+        wide = min(16 * per, classes - half - at)
+        delta_ref[:, at : at + wide] = predictions(1, i)[:, :wide]
+    change.wait()
+    res_ref[:, :half] = res_ref[:, :half] - (early[...] + late_ref[...])
 
 
 HOOKS = (
-    ("start", "ABC" + "AABAABCAABABCAABACABA"),
-    ((0, 0), "BC"),
-    ((0, 1), "BC"),
-    ((0, 2), "BCBCBBB"),
-    ((1, 0), "C"),
-    ((1, 1), "C"),
-    ((2, 0), "C"),
-    ((2, 1), "C"),
-    ((3, 0), "CC"),
-    ((3, 2), "CCCCCR"),
-    ((5, 0), "R"),
+    ("start", "ABCO" + "ABC" * 12),
+    ((0, 0), "R"),
+    ((2, 0), "R"),
+    ((4, 0), "R"),
     ((6, 0), "R"),
     ((7, 0), "R"),
     ((8, 0), "R"),
     ((9, 0), "R"),
-    ((10, 0), "RR"),
 )
 
 
-def sweep_over_all_rows(phi, own, labels, own_weights, padded):
+def sweep_over_all_rows(phi, weights, labels, padded):
     rows, n = phi.shape
-    classes = own.shape[1]
+    classes = weights.shape[0]
     total = packed_rows(n)
-    per = padded >> STAGES
-    blocks = (2,) * STAGES + (per, n)
+    per = padded >> (STAGES + 1)
+    blocks = (2,) * (STAGES + 1) + (per, n)
     vmem = pl.BlockSpec(memory_space=pltpu.VMEM)
     sem = pltpu.SemaphoreType.DMA
     f32, bf16 = jnp.float32, jnp.bfloat16
-    solution, residual = pl.pallas_call(
+    solution, residual, delta = pl.pallas_call(
         sweep_kernel,
         out_shape=(
             jax.ShapeDtypeStruct(blocks, f32),
             jax.ShapeDtypeStruct((rows, classes), f32),
+            jax.ShapeDtypeStruct((rows, classes - padded // 2), f32),
         ),
-        in_specs=[vmem] * 4,
-        out_specs=(vmem, vmem),
+        in_specs=[vmem, pl.BlockSpec(memory_space=pl.ANY), vmem],
+        out_specs=(vmem, vmem, vmem),
         scratch_shapes=[
             pltpu.VMEM((n, rows), bf16),
             pltpu.VMEM((total, B), f32),
@@ -474,21 +531,27 @@
             pltpu.VMEM((total, B), f32),
             pltpu.VMEM(blocks, f32),
             pltpu.VMEM(blocks, f32),
+            pltpu.VMEM((padded, n), f32),
             pltpu.VMEM((rows, classes), f32),
+            pltpu.VMEM((rows, classes), f32),
+            pltpu.VMEM((rows, padded // 2), f32),
+            pltpu.VMEM((rows, padded // 2), f32),
             pltpu.VMEM((rows, padded), bf16),
             pltpu.VMEM((padded, rows), bf16),
             pltpu.VMEM((n, n), f32),
             pltpu.VMEM((3, B, n), bf16),
             pltpu.VMEM((3, B, B), bf16),
-            pltpu.VMEM((3 * per, n), bf16),
+            pltpu.VMEM((6 * per, n), bf16),
             pltpu.VMEM((B, B), f32),
             pltpu.VMEM((48, B), bf16),
             pltpu.VMEM((48, B), bf16),
             pltpu.VMEM((8, B), f32),
             pltpu.VMEM((72, B), f32),
-            sem((2,)),
+            sem((4,)),
+            sem,
             *[sem((3, COLORS, STAGES))] * 4,
-            *[sem((COLORS, STAGES))] * 4,
+            *[sem((COLORS, STAGES))] * 2,
+            *[sem((2, COLORS, STAGES))] * 2,
         ],
         compiler_params=pltpu.CompilerParams(
             vmem_limit_bytes=VMEM_LIMIT, collective_id=0, has_side_effects=True
@@ -497,8 +560,8 @@
             flops=2 * n * n * n, bytes_accessed=300_000_000, transcendentals=0
         ),
         name="sweep_over_all_rows",
-    )(phi, own, labels.reshape(rows, 1), own_weights)
-    return solution.reshape(padded, n), residual
+    )(phi, weights, labels.reshape(1, rows))
+    return solution.reshape(padded, n), residual, delta
 
 
 def body(inputs, labels, frequencies, phases, weights):
@@ -513,29 +576,14 @@
         + phases[None, :]
     )
     phi = (scale * jnp.cos(arg)).astype(jnp.bfloat16)
-    own = jnp.dot(phi, weights.astype(jnp.bfloat16), preferred_element_type=jnp.float32)
-    bits, _ = place()
-    piece = 0
-    for bit in bits:
-        piece = piece * 2 + bit
-    per = padded // 64
-    start = jnp.minimum(piece * per, classes - per)
-    beyond = piece * per - start
-    kept = lax.dynamic_slice(weights, (0, start), (width, per)).T
-    own_weights = jnp.zeros_like(kept)
-    for shift in sorted({max(0, p * per - (classes - per)) for p in range(64)}):
-        if shift < per:
-            moved = jnp.pad(kept[shift:, :], ((0, shift), (0, 0)))
-            own_weights = jnp.where(beyond == shift, moved, own_weights)
-
-    solution, residual = sweep_over_all_rows(phi, own, labels, own_weights, padded)
-    solution = solution[:classes]
-    step = DAMP * solution
-    delta = lax.dot_general(
-        phi, step.astype(jnp.bfloat16), (((1,), (1,)), ((), ())), preferred_element_type=jnp.float32
-    )
+    solution, residual, delta = sweep_over_all_rows(phi, weights.T, labels, padded)
+    step = DAMP * solution[:classes]
+    half = padded // 2
     change = delta + lax.ppermute(delta, "grp", swap)
-    return (weights + step.T, residual - change)
+    return (
+        weights + step.T,
+        jnp.concatenate([residual[:, :half], residual[:, half:] - change], axis=1),
+    )
 
 
 def solution(mesh):

time: 263 us -> 223 us (0.85)
  waiting for transfers between devices: 15.3 us -> 0.55 us
  Pallas kernels: 212 us -> 200 us
  matrix products: 17.3 us -> 8.97 us
  other arithmetic: 11.7 us -> 8.92 us
    ppermute x1, waiting for transfers between devices: 15.3 us -> 0.55 us  [body(): change = delta + lax.ppermute(delta, 'grp', swap)]
    pallas_call x1, Pallas kernels: 212 us -> 200 us  [sweep_over_all_rows(): pl.pallas_call(sweep_kernel, out_shape=(jax.ShapeDtypeStruct(blocks, f32)...]
    dot_general x2 -> x0, matrix products: 9.03 us -> none  [the longest x1 5.02 us: body(): jnp.dot(phi, weights.astype(jnp.bfloat16), preferred_element_type=jnp.flo...]
  transfers between devices with their start and end apart: 1 -> 1, of which waited for: 1 -> 1; matrix products, arithmetic and copies ran while one was open for 3% -> 4% of each run, Pallas kernels for 0% -> 0%
where the time goes in v3:
time: 223 us; the launch traced here: 222 us
  Pallas kernels  200 us (90%)
  matrix products  8.97 us (4%)
  other arithmetic  8.92 us (4%)
  local copies, waits for them, and re-layouts  2.28 us (1%)
    pallas_call x1, Pallas kernels, sweep_over_all_rows(): pl.pallas_call(sweep_kernel, out_shape=(jax.ShapeDtypeStruct(blocks, f32)...  200 us
    dot_general x1, matrix products, body(): jnp.dot(inputs.astype(jnp.float32), frequencies, precision=lax.Precision....  8.97 us
    add x1, other arithmetic, body(): weights + step.T  8.69 us
  transfers between devices with their start and end apart: 1, of which 1 were waited for; matrix products, arithmetic and copies ran while one was open for 4% of the time, Pallas kernels for 0%

profile of v3, /device:TPU:10, one launch (start us, length us, event | category | flops | bytes accessed | tf_op | source)
XLA Modules:
  0.0 222.3 jit_solution(10817455841713326546)
XLA Ops:
  0.6 0.0 copy-start
  0.6 0.9 copy-done
  1.6 9.0 %fusion.4.phi_ref = bf16[256,1536]{1,0:T(8,128)(2,1)} fusion(bf16[256,512]{1,0:T(8,128)(2,1)S(1)} %copy-done, f32[512,1536]{1,0:T(8,128)} %param.7, f32[1536]{0:T(1024)} %param.8), kind=kOutput, calls=%fused_computation.6 | convolution fusion | flops 2417098752 | bytes 4200448 | tf_op jit(solution)/shard_map/dot_general | solution.py:575
  10.6 200.0 %sweep_over_all_rows.1 = (f32[2,2,2,2,2,2,2,8,1536]{8,7,6,5,4,3,2,1,0:T(8,128)}, f32[256,1000]{1,0:T(8,128)}, f32[256,488]{1,0:T(8,128)}) custom-call(bf16[256,1536]{1,0:T(8,128)(2,1)} %fusion.4.phi_ref, f32[1000,1536]{1,0:T(8,128)} %bitcast.9, s32[1,256]{1,0:T(1,128)} %bitcast.11), custom_call_target="tpu_custom_call" | custom-call | flops 7247757312 | bytes 300000000 | tf_op jit(solution)/shard_map/sweep_over_all_rows/pallas_call | solution.py:518
  210.6 0.9 collective-permute-start
  211.5 0.0 copy-start.1
  211.5 0.0 copy-start.2
  211.5 8.7 %fusion.1 = f32[1536,1000]{0,1:T(8,128)} fusion(f32[1536,1000]{0,1:T(8,128)} %param.9, f32[1024,1536]{1,0:T(8,128)} %bitcast.10), kind=kLoop, calls=%fused_computation.2 | loop fusion | flops 3072000 | bytes 18432000 | tf_op jit(solution)/shard_map/add | solution.py:584
  220.2 0.0 copy-done.1
  220.3 0.6 collective-permute-done
  220.8 0.0 copy-done.2
  220.8 0.1 add_subtract_fusion
  221.0 0.1 pad_maximum_fusion
  221.1 1.3 copy.7
  (1 shorter events, 0.0 us)
Async XLA Ops:
  0.6 1.0 copy-start
  210.6 10.2 %collective-permute-start = (f32[256,488]{1,0:T(8,128)}, f32[256,488]{1,0:T(8,128)S(1)}, u32[]{:S(2)}, u32[]{:S(2)}) collective-permute-start(f32[256,488]{1,0:T(8,128)} %get-tuple-element.7), channel_id=1, source_target_pairs={{0,64},{64,0},{1,65},{65,1},{2,66},{66,2},{3,67},{67,3},{4,68},{68... | collective-permute-start | bytes 1499144 | tf_op jit(solution)/shard_map/ppermute | solution.py:582
  211.5 8.7 %copy-start.1 = (f32[256,1000]{1,0:T(8,128)S(1)}, f32[256,1000]{1,0:T(8,128)}, u32[]{:S(2)}) copy-start(f32[256,1000]{1,0:T(8,128)} %get-tuple-element.6) | copy-start | bytes 3072004
  211.5 9.3 %copy-start.2 = (f32[256,488]{1,0:T(8,128)S(1)}, f32[256,488]{1,0:T(8,128)}, u32[]{:S(2)}) copy-start(f32[256,488]{1,0:T(8,128)} %get-tuple-element.7) | copy-start | bytes 1499140

commit v4 on v3

--- a/solution.py
+++ b/solution.py
@@ -209,22 +209,24 @@
     bring = pltpu.make_async_copy(all_ref, held_ref.at[pl.ds(0, classes), :], copy_sem)
     bring.start()
     held_ref[classes:, :] = jnp.zeros((held_ref.shape[0] - classes, n), jnp.float32)
-    for j in range(count):
-        phit[block(j), :] = phi_ref[:, block(j)].T
-    for j in range(count):
-        gpart[offsets[j] : offsets[j + 1], :] = lax.dot_general(
-            phit[B * j :, :],
-            phit[block(j), :],
-            (((1,), (1,)), ((), ())),
-            preferred_element_type=jnp.float32,
-        )
-    gpart[offsets[-1] :, :] = jnp.zeros((total - offsets[-1], B), jnp.float32)
-
     barrier = pltpu.get_barrier_semaphore()
     pl.semaphore_signal(barrier, inc=1, device_id={"grp": 1 - group}, device_id_type=MESH)
     for partner in partners:
         pl.semaphore_signal(barrier, inc=1, device_id={"row": partner}, device_id_type=MESH)
-    pl.semaphore_wait(barrier, len(partners) + 1)
+    for j in range(count):
+        phit[block(j), :] = phi_ref[:, block(j)].T
+
+    def own_gram():
+        gpart[offsets[-1] :, :] = jnp.zeros((total - offsets[-1], B), jnp.float32)
+        for j in range(count):
+            gpart[offsets[j] : offsets[j + 1], :] = lax.dot_general(
+                phit[B * j :, :],
+                phit[block(j), :],
+                (((1,), (1,)), ((), ())),
+                preferred_element_type=jnp.float32,
+            )
+            if offsets[j] < 2048 <= offsets[j + 1] or offsets[j] < 6144 <= offsets[j + 1]:
+                yield
 
     swap = pltpu.make_async_remote_copy(
         src_ref=own_ref,
@@ -355,6 +357,7 @@
         B=gram_wave(1, 2048, 4096),
         C=gram_wave(2, 6144, total - 6144),
         O=own_prediction(),
+        G=own_gram(),
         R=rhs_sum(),
     )
 
@@ -368,6 +371,8 @@
     eye = (
         lax.broadcasted_iota(jnp.int32, (B, B), 0) == lax.broadcasted_iota(jnp.int32, (B, B), 1)
     ).astype(jnp.float32)
+    go("G")
+    pl.semaphore_wait(barrier, len(partners) + 1)
     go(hooks["start"])
     system = a_ref[:B, :] + RIDGE * eye
     for j in range(count):
@@ -495,7 +500,7 @@
 
 
 HOOKS = (
-    ("start", "ABCO" + "ABC" * 12),
+    ("start", "AGBGCO" + "ABC" * 12),
     ((0, 0), "R"),
     ((2, 0), "R"),
     ((4, 0), "R"),

time: 223 us -> 222 us (level)
  no operation moved by 1% of the time
where the time goes in v4:
time: 222 us
  Pallas kernels  200 us (90%)
  matrix products  8.97 us (4%)
  other arithmetic  8.92 us (4%)
  local copies, waits for them, and re-layouts  2.28 us (1%)
    pallas_call x1, Pallas kernels, sweep_over_all_rows(): pl.pallas_call(sweep_kernel, out_shape=(jax.ShapeDtypeStruct(blocks, f32)...  200 us
    dot_general x1, matrix products, body(): jnp.dot(inputs.astype(jnp.float32), frequencies, precision=lax.Precision....  8.97 us
    add x1, other arithmetic, body(): weights + step.T  8.69 us
  transfers between devices with their start and end apart: 1, of which 1 were waited for; matrix products, arithmetic and copies ran while one was open for 4% of the time, Pallas kernels for 0%

profile of v4, /device:TPU:10, one launch (start us, length us, event | category | flops | bytes accessed | tf_op | source)
XLA Modules:
  0.0 222.2 jit_solution(15630012818143886644)
XLA Ops:
  0.6 0.0 copy-start
  0.6 0.9 copy-done
  1.6 9.0 %fusion.4.phi_ref = bf16[256,1536]{1,0:T(8,128)(2,1)} fusion(bf16[256,512]{1,0:T(8,128)(2,1)S(1)} %copy-done, f32[512,1536]{1,0:T(8,128)} %param.7, f32[1536]{0:T(1024)} %param.8), kind=kOutput, calls=%fused_computation.6 | convolution fusion | flops 2417098752 | bytes 4200448 | tf_op jit(solution)/shard_map/dot_general | solution.py:580
  10.6 199.9 %sweep_over_all_rows.1 = (f32[2,2,2,2,2,2,2,8,1536]{8,7,6,5,4,3,2,1,0:T(8,128)}, f32[256,1000]{1,0:T(8,128)}, f32[256,488]{1,0:T(8,128)}) custom-call(bf16[256,1536]{1,0:T(8,128)(2,1)} %fusion.4.phi_ref, f32[1000,1536]{1,0:T(8,128)} %bitcast.9, s32[1,256]{1,0:T(1,128)} %bitcast.11), custom_call_target="tpu_custom_call" | custom-call | flops 7247757312 | bytes 300000000 | tf_op jit(solution)/shard_map/sweep_over_all_rows/pallas_call | solution.py:523
  210.4 0.8 collective-permute-start
  211.3 0.0 copy-start.1
  211.3 0.0 copy-start.2
  211.3 8.7 %fusion.1 = f32[1536,1000]{0,1:T(8,128)} fusion(f32[1536,1000]{0,1:T(8,128)} %param.9, f32[1024,1536]{1,0:T(8,128)} %bitcast.10), kind=kLoop, calls=%fused_computation.2 | loop fusion | flops 3072000 | bytes 18432000 | tf_op jit(solution)/shard_map/add | solution.py:589
  220.0 0.0 copy-done.1
  220.0 0.7 collective-permute-done
  220.7 0.0 copy-done.2
  220.7 0.1 add_subtract_fusion
  220.8 0.1 pad_maximum_fusion
  220.9 1.3 copy.7
  (1 shorter events, 0.0 us)
Async XLA Ops:
  0.6 1.0 copy-start
  210.4 10.2 %collective-permute-start = (f32[256,488]{1,0:T(8,128)}, f32[256,488]{1,0:T(8,128)S(1)}, u32[]{:S(2)}, u32[]{:S(2)}) collective-permute-start(f32[256,488]{1,0:T(8,128)} %get-tuple-element.7), channel_id=1, source_target_pairs={{0,64},{64,0},{1,65},{65,1},{2,66},{66,2},{3,67},{67,3},{4,68},{68... | collective-permute-start | bytes 1499144 | tf_op jit(solution)/shard_map/ppermute | solution.py:587
  211.3 8.7 %copy-start.1 = (f32[256,1000]{1,0:T(8,128)S(1)}, f32[256,1000]{1,0:T(8,128)}, u32[]{:S(2)}) copy-start(f32[256,1000]{1,0:T(8,128)} %get-tuple-element.6) | copy-start | bytes 3072004
  211.3 9.4 %copy-start.2 = (f32[256,488]{1,0:T(8,128)S(1)}, f32[256,488]{1,0:T(8,128)}, u32[]{:S(2)}) copy-start(f32[256,488]{1,0:T(8,128)} %get-tuple-element.7) | copy-start | bytes 1499140
